TPU v7x, 256 devices: a whole 4x4x8 slice. The times are simulated.
256 devices in a mesh: rows: 32 (over x, z), dim: 8 (over y, core).
Axes of the slice: x: 4, y: 4, z: 8, core: 2. Of those that a mesh axis runs over, the one named last changes fastest.
Arguments:
- embeddings: float32 [256, 512, 128], P('rows', 'dim'), as said below
- prior: float32 [256, 512, 128], P('rows', 'dim'), may hold values from -9 to 9
- neighbours: int32 [256, 16], P('rows'), may hold values from 0 to 255, as said below
- seed_mask: int32 [32768], P('rows'), may hold values 0 or 1
- families: int32 [32768], P('rows'), may hold values from 0 to 511
Outputs:
- log_ratio: float32 [32768, 512], P(('rows', 'dim'))
Inputs may be any that keep to these rules, and one draw needn't show every extreme that they name: `neighbours`: each list names 16 different blocks. Together, the lists of the 8 blocks 8g to 8g + 7 of one group name exactly 2 different blocks of every group of 8 blocks. `embeddings`: each row has its own positive scale.
All inputs are finite; a program needn't handle non-finite values. No bound on the sum of `seed_mask` on one device may be relied on, other than what follows from the above.
Results may differ from a plain program's by a relative error of at most 0.00078.
Values may be sent and summed in bfloat16 or wider, within the bound.
No kernel may reach another device: no remote copies, remote signals or barrier semaphores. Data moves between devices by JAX's collectives and lax.ppermute only.
A program may use at most 64 MiB of HBM per device.

v0:
```python
import jax
import jax.numpy as jnp
from jax import lax
from jax.sharding import PartitionSpec as P

ITERS = 3


sharpness = 16.0
seed_weight = 0.5
label_floor = 0.001
norm_eps = 1e-06


def shards(embeddings, prior, neighbours, seed_mask, families):
    groups = lax.axis_size("rows")
    splits = lax.axis_size("dim")
    member = lax.axis_index("dim")
    blocks = neighbours.shape[0]
    links = neighbours.shape[1]
    width = embeddings.shape[1]
    block_rows = embeddings.shape[2]
    fam_part = prior.shape[1]
    fam_all = fam_part * splits
    slots = blocks // 4
    owned = blocks // splits
    local_squares = jnp.sum(embeddings * embeddings, axis=1)
    raised_prior = jnp.exp(prior)
    local_total = jnp.sum(raised_prior, axis=1)
    squares, prior_total = lax.psum((local_squares, local_total), "dim")
    unit_blocks = embeddings * lax.rsqrt(squares + norm_eps)[:, None, :]
    labels = (raised_prior / prior_total[:, None, :]).astype(jnp.bfloat16)
    everything = groups * blocks
    hits = neighbours[:, :, None] == jnp.arange(everything, dtype=jnp.int32)[None, None, :]
    named = jnp.any(hits, axis=(0, 1)).reshape(groups, blocks)
    places = jnp.arange(blocks, dtype=jnp.int32)
    ranked = jnp.argsort(jnp.where(named, places[None, :], blocks + places[None, :]), axis=1)[
        :, :slots
    ]
    wanted = lax.all_to_all(ranked, "rows", split_axis=0, concat_axis=0, tiled=True)
    owner = neighbours // blocks
    within = neighbours % blocks
    owner_slots = ranked[owner]
    match = (owner_slots == within[:, :, None]).astype(jnp.int32)
    position = jnp.sum(match * jnp.arange(slots, dtype=jnp.int32)[None, None, :], axis=2)
    flat = owner * slots + position
    outgoing = unit_blocks[wanted]
    arrived = lax.all_to_all(outgoing, "rows", split_axis=0, concat_axis=0, tiled=True).reshape(
        groups * slots, width, block_rows
    )
    keys = arrived[flat]
    products = jnp.einsum(
        "qer,qlek->qrlk",
        unit_blocks,
        keys,
        precision=lax.Precision.HIGHEST,
        preferred_element_type=jnp.float32,
    )
    cosine = lax.psum_scatter(
        products.reshape(owned * lax.axis_size("dim"), block_rows, links * block_rows),
        "dim",
        scatter_dimension=0,
        tiled=True,
    )
    raised = jnp.exp(sharpness * (cosine - 1.0))
    weights = (raised / jnp.sum(raised, axis=2, keepdims=True)).astype(jnp.bfloat16)
    weights = weights.reshape(owned, block_rows, links, block_rows)
    first_row = member * owned * block_rows
    my_seeds = lax.dynamic_slice_in_dim(seed_mask, first_row, owned * block_rows, 0)
    my_families = lax.dynamic_slice_in_dim(families, first_row, owned * block_rows, 0)
    onehot = (my_families[:, None] == jnp.arange(fam_all, dtype=jnp.int32)[None, :]).astype(
        jnp.float32
    )
    seeds = (seed_weight * my_seeds.astype(jnp.float32)[:, None] * onehot).reshape(
        owned, block_rows, fam_all
    )
    shifted = seeds
    total = seeds
    for sweep in range(ITERS):
        sending = labels[wanted]
        came = lax.all_to_all(sending, "rows", split_axis=0, concat_axis=0, tiled=True).reshape(
            groups * slots, fam_part, block_rows
        )
        near = came[flat]
        gathered = lax.all_to_all(near, "dim", split_axis=0, concat_axis=2, tiled=True)
        mixed = (
            jnp.einsum("qrlk,qlfk->qrf", weights, gathered, preferred_element_type=jnp.float32)
            + seeds
        )
        shifted = mixed + label_floor
        squared = shifted * shifted
        total = jnp.sum(squared, axis=2, keepdims=True)
        if sweep + 1 < ITERS:
            fresh = jnp.transpose((squared / total).astype(jnp.bfloat16), (0, 2, 1))
            labels = lax.all_to_all(fresh, "dim", split_axis=1, concat_axis=0, tiled=True)
    result = 2.0 * jnp.log(shifted) - jnp.log(total) + jnp.log(jnp.float32(fam_all))
    return result.reshape(owned * block_rows, fam_all)


def solution(mesh):
    return jax.shard_map(
        shards,
        mesh=mesh,
        in_specs=(
            P("rows", "dim", None),
            P("rows", "dim", None),
            P("rows", None),
            P("rows"),
            P("rows"),
        ),
        out_specs=P(("rows", "dim"), None),
        check_vma=False,
    )
```

profile of v0, /device:TPU:1, one launch (start us, length us, event | category | flops | bytes accessed | tf_op | source)
XLA Modules:
  0.0 364.3 jit_solution(8177645556907649418)
XLA Ops:
  8.9 11.9 %all-to-all-start = ((s32[32,1,2]{2,1,0:T(1,128)}), s32[32,1,2]{2,1,0:T(1,128)S(1)}, u32[]{:S(2)}, u32[]{:S(2)}) async-start(s32[32,1,2]{2,1,0:T(1,128)} %bitcast.37), calls=%async_computation | async-start | bytes 32768 | tf_op jit(solution)/shard_map/all_to_all | solution.py:40
  20.8 1.1 multiply_reduce_fusion.1
  21.9 13.4 %all-reduce = (f32[8,128]{1,0:T(8,128)S(1)}, f32[8,128]{1,0:T(8,128)S(1)}) all-reduce(f32[8,128]{1,0:T(8,128)S(1)} %get-tuple-element.17, f32[8,128]{1,0:T(8,128)S(1)} %get-tuple-element.18), channel_id=1, replica_groups=mesh['rows'=32,'dim'=8] {'dim'}, use_global_device_ids=true, to_apply=%region_1.0 | all-reduce | flops 2048 | bytes 16384 | tf_op jit(solution)/shard_map/psum | solution.py:30
  35.3 1.0 broadcast_multiply_fusion
  36.6 2.0 gather_fusion
  38.7 9.3 %all-to-all-start.1 = ((f32[32,2,64,128]{3,2,1,0:T(8,128)}), f32[32,2,64,128]{3,2,1,0:T(8,128)S(1)}, u32[]{:S(2)}, u32[]{:S(2)}) async-start(f32[32,2,64,128]{3,2,1,0:T(8,128)} %bitcast.95), calls=%async_computation.1 | async-start | bytes 4194304 | tf_op jit(solution)/shard_map/all_to_all | solution.py:48
  48.2 1.4 gather_fusion.1
  49.9 46.9 %all-to-all-done.1 = f32[32,2,64,128]{3,2,1,0:T(8,128)S(1)} async-done(((f32[32,2,64,128]{3,2,1,0:T(8,128)}), f32[32,2,64,128]{3,2,1,0:T(8,128)S(1)}, u32[]{:S(2)}, u32[]{:S(2)}) %all-to-all-start.1) | async-done | bytes 2097184 | tf_op jit(solution)/shard_map/all_to_all | solution.py:48
  96.9 2.8 gather_fusion.2
  99.7 16.9 %fusion.9 = f32[8,128,16,128]{1,3,2,0:T(8,128)} fusion(f32[8,16,64,128]{3,2,1,0:T(8,128)} %bitcast.86, f32[8,64,128]{2,1,0:T(8,128)S(1)} %broadcast_multiply_fusion), kind=kOutput, calls=%fused_computation.23 | convolution fusion | flops 1610612736 | bytes 12845056 | tf_op jit(solution)/shard_map/qer,qlek->qrlk/dot_general | solution.py:52
  116.6 0.9 copy-done.4
  118.4 28.6 %all_to_all.101 = bf16[32,2,64,128]{3,2,1,0:T(8,128)(2,1)S(1)} all-to-all(bf16[32,2,64,128]{3,2,1,0:T(8,128)(2,1)S(1)} %bitcast.105), channel_id=1, replica_groups=mesh['rows'=32,'dim'=8] {'rows'}, dimensions={0} | all-to-all | bytes 2097152 | tf_op jit(solution)/shard_map/all_to_all | solution.py:81
  146.9 2.2 gather_fusion.4
  149.1 12.2 %all-to-all-start.3 = ((bf16[8,16,64,128]{3,2,1,0:T(8,128)(2,1)}), bf16[8,16,64,128]{3,2,1,0:T(8,128)(2,1)S(1)}, u32[]{:S(2)}, u32[]{:S(2)}) async-start(bf16[8,16,64,128]{3,2,1,0:T(8,128)(2,1)} %bitcast.13), calls=%async_computation.4 | async-start | bytes 4194304 | tf_op jit(solution)/shard_map/all_to_all | solution.py:85
  162.8 28.9 %all-to-all-done.3 = bf16[8,16,64,128]{3,2,1,0:T(8,128)(2,1)S(1)} async-done(((bf16[8,16,64,128]{3,2,1,0:T(8,128)(2,1)}), bf16[8,16,64,128]{3,2,1,0:T(8,128)(2,1)S(1)}, u32[]{:S(2)}, u32[]{:S(2)}) %all-to-all-start.3) | async-done | bytes 2097184 | tf_op jit(solution)/shard_map/all_to_all | solution.py:85
  191.7 1.6 copy.40
  193.4 1.7 fusion.8
  195.0 1.4 divide_convert_fusion
  196.5 0.9 fusion.16
  198.2 1.4 reduce.7
  199.6 8.5 %all_to_all.102 = bf16[8,2,4096]{2,1,0:T(2,128)(2,1)S(1)} all-to-all(bf16[8,2,4096]{2,1,0:T(2,128)(2,1)S(1)} %reshape.234), channel_id=1, replica_groups=mesh['rows'=32,'dim'=8] {'dim'}, dimensions={0} | all-to-all | bytes 262144 | tf_op jit(solution)/shard_map/all_to_all | solution.py:95
  209.1 34.2 %all_to_all.103 = bf16[32,2,64,128]{3,2,1,0:T(8,128)(2,1)S(1)} all-to-all(bf16[32,2,64,128]{3,2,1,0:T(8,128)(2,1)S(1)} %bitcast.106), channel_id=1, replica_groups=mesh['rows'=32,'dim'=8] {'rows'}, dimensions={0} | all-to-all | bytes 2097152 | tf_op jit(solution)/shard_map/all_to_all | solution.py:81
  243.3 0.9 gather_fusion.6
  244.2 33.5 %all_to_all.104 = bf16[8,16,64,128]{3,2,1,0:T(8,128)(2,1)S(1)} all-to-all(bf16[8,16,64,128]{3,2,1,0:T(8,128)(2,1)S(1)} %bitcast.93), channel_id=1, replica_groups=mesh['rows'=32,'dim'=8] {'dim'}, dimensions={0} | all-to-all | bytes 4194304 | tf_op jit(solution)/shard_map/all_to_all | solution.py:85
  278.7 0.9 fusion.17
  279.9 1.4 reduce.8
  281.4 8.7 %all_to_all.105 = bf16[8,2,4096]{2,1,0:T(2,128)(2,1)S(1)} all-to-all(bf16[8,2,4096]{2,1,0:T(2,128)(2,1)S(1)} %reshape.236), channel_id=1, replica_groups=mesh['rows'=32,'dim'=8] {'dim'}, dimensions={0} | all-to-all | bytes 262144 | tf_op jit(solution)/shard_map/all_to_all | solution.py:95
  290.9 29.3 %all_to_all.106 = bf16[32,2,64,128]{3,2,1,0:T(8,128)(2,1)S(1)} all-to-all(bf16[32,2,64,128]{3,2,1,0:T(8,128)(2,1)S(1)} %bitcast.104), channel_id=1, replica_groups=mesh['rows'=32,'dim'=8] {'rows'}, dimensions={0} | all-to-all | bytes 2097152 | tf_op jit(solution)/shard_map/all_to_all | solution.py:81
  320.3 0.9 gather_fusion.8
  321.2 33.5 %all_to_all.107 = bf16[8,16,64,128]{3,2,1,0:T(8,128)(2,1)S(1)} all-to-all(bf16[8,16,64,128]{3,2,1,0:T(8,128)(2,1)S(1)} %bitcast.92), channel_id=1, replica_groups=mesh['rows'=32,'dim'=8] {'dim'}, dimensions={0} | all-to-all | bytes 4194304 | tf_op jit(solution)/shard_map/all_to_all | solution.py:85
  355.7 0.9 multiply_reduce_fusion
  356.6 0.8 subtract_add_fusion
  (56 shorter events, 10.5 us)
Async XLA Ops:
  8.9 27.4 %all-to-all-start = ((s32[32,1,2]{2,1,0:T(1,128)}), s32[32,1,2]{2,1,0:T(1,128)S(1)}, u32[]{:S(2)}, u32[]{:S(2)}) async-start(s32[32,1,2]{2,1,0:T(1,128)} %bitcast.37), calls=%async_computation | async-start | bytes 32768 | tf_op jit(solution)/shard_map/all_to_all | solution.py:40
  38.7 9.4 %copy-start.5 = (s32[8,16]{1,0:T(8,128)S(1)}, s32[8,16]{1,0:T(8,128)}, u32[]{:S(2)}) copy-start(s32[8,16]{1,0:T(8,128)} %param.7) | copy-start | bytes 1540
  38.7 58.2 %all-to-all-start.1 = ((f32[32,2,64,128]{3,2,1,0:T(8,128)}), f32[32,2,64,128]{3,2,1,0:T(8,128)S(1)}, u32[]{:S(2)}, u32[]{:S(2)}) async-start(f32[32,2,64,128]{3,2,1,0:T(8,128)} %bitcast.95), calls=%async_computation.1 | async-start | bytes 4194304 | tf_op jit(solution)/shard_map/all_to_all | solution.py:48
  48.0 145.4 %reduce-scatter.2.cloned.1.call-start = ((), (), s32[]{:S(2)}) async-start(), calls=%async_computation.11 | async-start | bytes 9437184 | tf_op jit(solution)/shard_map/reduce_scatter | solution.py:59
  116.6 0.9 copy-start.4
  149.1 42.6 %all-to-all-start.3 = ((bf16[8,16,64,128]{3,2,1,0:T(8,128)(2,1)}), bf16[8,16,64,128]{3,2,1,0:T(8,128)(2,1)S(1)}, u32[]{:S(2)}, u32[]{:S(2)}) async-start(bf16[8,16,64,128]{3,2,1,0:T(8,128)(2,1)} %bitcast.13), calls=%async_computation.4 | async-start | bytes 4194304 | tf_op jit(solution)/shard_map/all_to_all | solution.py:85
  193.4 3.1 copy-start
  196.5 0.9 copy-start.1
  277.7 1.0 copy-start.2
  354.7 1.0 copy-start.3
Sparse Core Ops, SparseCore 0:
  116.7 61.2 reduce-scatter.1
where the time goes:
time: 365 us; the launch traced here: 364 us
  blocking collectives  190 us (52%)
  waiting for transfers between devices  75.9 us (21%)
  starting transfers between devices  33.4 us (9%)
  local copies, waits for them, and re-layouts  20.4 us (6%)
  matrix products  19.7 us (5%)
  between operations  13.7 us (4%)
  other arithmetic  11.7 us (3%)
    all_to_all x3, blocking collectives, shards(): lax.all_to_all(sending, 'rows', split_axis=0, concat_axis=0, tiled=True)  92.1 us
    all_to_all x2, blocking collectives, shards(): lax.all_to_all(near, 'dim', split_axis=0, concat_axis=2, tiled=True)  66.9 us
    all_to_all x1, waiting for transfers between devices, shards(): lax.all_to_all(outgoing, 'rows', split_axis=0, concat_axis=0, tiled=True)  46.9 us
    all_to_all x1, waiting for transfers between devices, shards(): lax.all_to_all(near, 'dim', split_axis=0, concat_axis=2, tiled=True)  28.9 us
    all_to_all x2, blocking collectives, shards(): lax.all_to_all(fresh, 'dim', split_axis=1, concat_axis=0, tiled=True)  17.2 us
    dot_general x1, matrix products, shards(): jnp.einsum('qer,qlek->qrlk', unit_blocks, keys, precision=lax.Precision.H...  16.9 us
    psum x1, blocking collectives, shards(): squares, prior_total = lax.psum((local_squares, local_total), 'dim')  13.4 us
    all_to_all x1, starting transfers between devices, shards(): lax.all_to_all(near, 'dim', split_axis=0, concat_axis=2, tiled=True)  12.2 us
  transfers between devices with their start and end apart: 4, of which 2 were waited for; matrix products, arithmetic and copies ran while one was open for 3% of the time, Pallas kernels for 0%

commit v1 on v0

v1 whole, which is shorter than its diff:
```python
import jax
import jax.numpy as jnp
from jax import lax
from jax.experimental import pallas as pl
from jax.experimental.pallas import tpu as pltpu
from jax.sharding import PartitionSpec as P

ITERS = 3
CORES = 2

sharpness = 16.0
seed_weight = 0.5
label_floor = 0.001
norm_eps = 1e-06

F32 = jnp.float32
BF16 = jnp.bfloat16
SMEM = pl.BlockSpec(memory_space=pltpu.SMEM)
VMEM = pl.BlockSpec(memory_space=pltpu.VMEM)


def call(body, outs, specs, *args, scratch=()):
    return pl.pallas_call(
        body,
        out_shape=outs,
        in_specs=specs,
        out_specs=jax.tree.map(lambda _: VMEM, outs),
        scratch_shapes=scratch,
    )(*args)


def raise_prior(prior):
    blocks, fams, rows = prior.shape
    parts = 4

    def body(prior_ref, out_ref):
        for pair in range(blocks // 2):
            both = jnp.exp(prior_ref[2 * pair : 2 * pair + 2]).reshape(2 * fams, rows)
            out_ref[:, pair] = both.T.reshape(parts, rows // parts, 2 * fams)

    return call(
        body,
        jax.ShapeDtypeStruct((parts, blocks // 2, rows // parts, 2 * fams), F32),
        [VMEM],
        prior,
    )


def lanes_of(column):
    return jnp.broadcast_to(column, (column.shape[0], 128)).T[:8]


def column_of(lanes):
    return jnp.broadcast_to(lanes[:1], (128, lanes.shape[1])).T


def gather_prior(came):
    sources, pairs, rows, both = came.shape
    fams = both // 2

    def body(came_ref, out_ref, total_ref):
        for pair in range(pairs):
            for half in range(2):
                wide = jnp.concatenate(
                    [came_ref[s, pair][:, half * fams : half * fams + fams] for s in range(sources)],
                    axis=1,
                )
                out_ref[2 * pair + half] = wide
        whole = out_ref[...].reshape(2 * pairs * rows, sources * fams)
        total_ref[...] = lanes_of(jnp.sum(whole, axis=1, keepdims=True))

    return call(
        body,
        (
            jax.ShapeDtypeStruct((2 * pairs, rows, sources * fams), F32),
            jax.ShapeDtypeStruct((8, 2 * pairs * rows), F32),
        ),
        [VMEM],
        came,
    )


def pick_embeddings(everyone, wanted, first):
    sources, blocks, feats, rows = everyone.shape
    count = wanted.shape[0]
    part = rows // 4

    def body(every_ref, wanted_ref, first_ref, rows_ref, out_ref):
        for block in range(blocks):
            wide = every_ref[:, block].astype(F32).reshape(sources * feats, rows)
            rows_ref[block] = wide.T.astype(BF16)
        start = pl.multiple_of(first_ref[0], part)

        def one(slot, carry):
            out_ref[slot] = rows_ref[wanted_ref[slot], pl.ds(start, part), :]
            return carry

        lax.fori_loop(0, count, one, 0, unroll=8)

    return call(
        body,
        (
            jax.ShapeDtypeStruct((blocks, rows, sources * feats), BF16),
            jax.ShapeDtypeStruct((count, part, sources * feats), BF16),
        ),
        [VMEM, SMEM, SMEM],
        everyone,
        wanted,
        first,
    )


def pick_labels(squared, total, other, wanted):
    blocks, part, fams = squared.shape
    count = wanted.shape[0]

    def body(squared_ref, total_ref, other_ref, wanted_ref, out_ref, labels_ref):
        whole = column_of(total_ref[...] + other_ref[...])
        for block in range(blocks):
            down = whole[block * part : block * part + part]
            down = jnp.concatenate([down] * (fams // 128), axis=1)
            labels_ref[block] = (squared_ref[block] / down).astype(BF16)

        def one(slot, carry):
            out_ref[slot] = labels_ref[wanted_ref[slot]]
            return carry

        lax.fori_loop(0, count, one, 0, unroll=8)

    return call(
        body,
        jax.ShapeDtypeStruct((count, part, fams), BF16),
        [VMEM, VMEM, VMEM, SMEM],
        squared,
        total,
        other,
        wanted,
        scratch=[pltpu.VMEM((blocks, part, fams), BF16)],
    )


def raise_cosines(queries, queries_other, keys, keys_other, flat):
    blocks, rows, feats = queries.shape
    slots, part, _ = keys.shape
    links = flat.shape[0] // blocks

    def body(q_ref, qo_ref, k_ref, ko_ref, flat_ref, out_ref, sum_ref, a_ref, b_ref, n_ref, inv_ref):
        def norm(first, second):
            first, second = first.astype(F32), second.astype(F32)
            squares = jnp.sum(first * first + second * second, axis=1, keepdims=True)
            return lax.rsqrt(squares + norm_eps)

        step = 8
        for at in range(0, slots, step):
            inverse = norm(
                k_ref[at : at + step].reshape(step * part, feats),
                ko_ref[at : at + step].reshape(step * part, feats),
            )
            inv_ref[at : at + step] = jnp.broadcast_to(inverse, (step * part, rows)).reshape(
                step, part, rows
            )
        for block in range(blocks):
            for link in range(links):
                slot = flat_ref[block * links + link]
                a_ref[link * part : link * part + part] = k_ref[slot]
                b_ref[link * part : link * part + part] = ko_ref[slot]
                n_ref[link * part : link * part + part] = inv_ref[slot]
            first, second = q_ref[block], qo_ref[block]
            inverse = jnp.broadcast_to(norm(first, second), (rows, rows)).T[:1]
            dims = (((1,), (1,)), ((), ()))
            product = lax.dot_general(a_ref[...], first, dims, preferred_element_type=F32)
            product += lax.dot_general(b_ref[...], second, dims, preferred_element_type=F32)
            raised = jnp.exp(sharpness * (product * n_ref[...] * inverse - 1.0))
            out_ref[block] = raised
            sum_ref[block : block + 1] = jnp.sum(raised, axis=0, keepdims=True)

    return call(
        body,
        (
            jax.ShapeDtypeStruct((blocks, links * part, rows), F32),
            jax.ShapeDtypeStruct((blocks, rows), F32),
        ),
        [VMEM, VMEM, VMEM, VMEM, SMEM],
        queries,
        queries_other,
        keys,
        keys_other,
        flat,
        scratch=[
            pltpu.VMEM((links * part, feats), BF16),
            pltpu.VMEM((links * part, feats), BF16),
            pltpu.VMEM((links * part, rows), F32),
            pltpu.VMEM((slots, part, rows), F32),
        ],
    )


def weigh(raised, sums):
    blocks, keys, rows = raised.shape

    def body(raised_ref, sums_ref, out_ref):
        total = jnp.sum(sums_ref[...], axis=0)
        for block in range(blocks):
            out_ref[block] = (raised_ref[block] / total[block : block + 1]).T.astype(BF16)

    return call(
        body, jax.ShapeDtypeStruct((blocks, rows, keys), BF16), [VMEM, VMEM], raised, sums
    )


def mix(weights, near, flat, by_slice):
    blocks, rows, keys = weights.shape
    _, part, fams = near.shape
    links = flat.shape[0] // blocks
    slices = rows // part

    def body(weights_ref, near_ref, flat_ref, out_ref, l_ref):
        for block in range(blocks):
            for link in range(links):
                slot = flat_ref[block * links + link]
                l_ref[link * part : link * part + part] = near_ref[slot]
            mixed = jnp.dot(weights_ref[block], l_ref[...], preferred_element_type=F32)
            mixed = mixed.astype(BF16)
            if by_slice:
                out_ref[:, block] = mixed.reshape(slices, part, fams)
            else:
                out_ref[block] = mixed

    shape = (slices, blocks, part, fams) if by_slice else (blocks, rows, fams)
    return call(
        body,
        jax.ShapeDtypeStruct(shape, BF16),
        [VMEM, VMEM, SMEM],
        weights,
        near,
        flat,
        scratch=[pltpu.VMEM((keys, fams), BF16)],
    )


def square(parts, seeds):
    sources, blocks, part, fams = parts.shape

    def body(parts_ref, seeds_ref, out_ref, total_ref):
        mixed = parts_ref[0].astype(F32)
        for source in range(1, sources):
            mixed += parts_ref[source].astype(F32)
        shifted = mixed + seeds_ref[...] + label_floor
        squared = shifted * shifted
        out_ref[...] = squared
        whole = squared.reshape(blocks * part, fams)
        total_ref[...] = lanes_of(jnp.sum(whole, axis=1, keepdims=True))

    return call(
        body,
        (
            jax.ShapeDtypeStruct((blocks, part, fams), F32),
            jax.ShapeDtypeStruct((8, blocks * part), F32),
        ),
        [VMEM, VMEM],
        parts,
        seeds,
    )


def finish(parts, seeds, slab):
    members, rows, fams = parts.shape

    def body(parts_ref, seeds_ref, out_ref):
        halves = []
        for core in range(CORES):
            mixed = parts_ref[core].astype(F32)
            for source in range(core + CORES, members, CORES):
                mixed += parts_ref[source].astype(F32)
            halves.append(mixed + seeds_ref[core] + label_floor)
        total = sum(jnp.sum(half * half, axis=1, keepdims=True) for half in halves)
        last = jnp.log(F32(CORES * fams)) - jnp.log(total)
        for at in range(fams // slab):
            wide = jnp.concatenate(
                [half[:, at * slab : at * slab + slab] for half in halves], axis=1
            )
            out_ref[:, at * CORES * slab : (at + 1) * CORES * slab] = 2.0 * jnp.log(wide) + last

    return call(
        body, jax.ShapeDtypeStruct((rows, CORES * fams), F32), [VMEM, VMEM], parts, seeds
    )


def shards(embeddings, prior, neighbours, seed_mask, families):
    groups = lax.axis_size("rows")
    members = lax.axis_size("dim")
    member = lax.axis_index("dim")
    blocks, links = neighbours.shape
    slab = embeddings.shape[1]
    rows = embeddings.shape[2]
    sides = members // CORES
    side, core = member // CORES, member % CORES
    part = rows // sides
    lines = [[s * CORES + k for s in range(sides)] for k in range(CORES)]
    swap = [(m, m ^ 1) for m in range(members)]

    def over_y(x):
        return lax.all_to_all(
            x, "dim", split_axis=0, concat_axis=0, tiled=True, axis_index_groups=lines
        )

    def over_rows(x):
        return lax.all_to_all(x, "rows", split_axis=0, concat_axis=0, tiled=True)

    def other_core(x):
        return lax.ppermute(x, "dim", swap)

    def across(out):
        return over_rows(out.reshape(groups, out.shape[0] // groups, *out.shape[1:])).reshape(
            out.shape
        )

    lists = neighbours.reshape(blocks * links)
    owner, within = lists // blocks, lists % blocks
    held = owner[None, :] == jnp.arange(groups, dtype=jnp.int32)[:, None]
    low = jnp.min(jnp.where(held, within[None, :], blocks), axis=1)
    high = jnp.max(jnp.where(held, within[None, :], -1), axis=1)
    wanted = over_rows(jnp.stack([low, high], axis=1)).reshape(groups * 2)
    highs = jnp.sum(jnp.where(held, high[:, None], 0), axis=0)
    flat = owner * 2 + (within == highs).astype(jnp.int32)

    rounded = embeddings.astype(BF16)
    everyone = over_y(jnp.broadcast_to(rounded[None], (sides, *rounded.shape)))
    first = (side * part).reshape(1)
    queries, outgoing = pick_embeddings(everyone, wanted, first)
    keys = across(outgoing)
    queries_other = other_core(queries)

    raised_prior, total = gather_prior(over_y(raise_prior(prior)))
    near = across(pick_labels(raised_prior, total, other_core(total), wanted))

    keys_other = other_core(keys)
    raised, sums = raise_cosines(queries, queries_other, keys, keys_other, flat)
    weights = weigh(raised, over_y(jnp.broadcast_to(sums[None], (sides, *sums.shape))))

    at = jnp.arange(sides * slab, dtype=jnp.int32)
    ids = (at // slab) * (CORES * slab) + at % slab

    def seeded(mask, fams, core):
        return (
            seed_weight
            * mask.astype(F32)[..., None]
            * (fams[..., None] == ids + core * slab).astype(F32)
        )

    mask = seed_mask.reshape(blocks, rows)
    fams = families.reshape(blocks, rows)
    seeds = seeded(
        lax.dynamic_slice_in_dim(mask, side * part, part, 1),
        lax.dynamic_slice_in_dim(fams, side * part, part, 1),
        core,
    )
    my_mask = lax.dynamic_index_in_dim(mask, member, 0, keepdims=False)
    my_fams = lax.dynamic_index_in_dim(fams, member, 0, keepdims=False)
    my_seeds = jnp.stack([seeded(my_mask, my_fams, k) for k in range(CORES)])

    for sweep in range(ITERS - 1):
        squared, total = square(over_y(mix(weights, near, flat, True)), seeds)
        near = across(pick_labels(squared, total, other_core(total), wanted))
    parts = lax.all_to_all(
        mix(weights, near, flat, False), "dim", split_axis=0, concat_axis=0, tiled=True
    )
    return finish(parts, my_seeds, slab)


def solution(mesh):
    return jax.shard_map(
        shards,
        mesh=mesh,
        in_specs=(
            P("rows", "dim", None),
            P("rows", "dim", None),
            P("rows", None),
            P("rows"),
            P("rows"),
        ),
        out_specs=P(("rows", "dim"), None),
        check_vma=False,
    )
```

time: 365 us -> 266 us (0.73)
  blocking collectives: 190 us -> 67.8 us
  Pallas kernels: 0 us -> 34.9 us
  starting transfers between devices: 33.4 us -> 67 us
  matrix products: 19.7 us -> 0 us
  between operations: 13.7 us -> 0.16 us
  other arithmetic: 11.7 us -> 4.19 us
  local copies, waits for them, and re-layouts: 20.4 us -> 12.9 us
    all_to_all x7 -> x3, blocking collectives: 176 us -> 67.8 us  [the longest x2 56.7 us: over_rows(): return lax.all_to_all(x, 'rows', split_axis=0, concat_axis=0, tiled=True)]
    pallas_call x0 -> x14, Pallas kernels: none -> 34.9 us  [call(): pl.pallas_call(body, out_shape=outs, in_specs=specs, out_specs=jax.tree.m...]
    ppermute x0 -> x5, starting transfers between devices: none -> 20.3 us  [other_core(): return lax.ppermute(x, 'dim', swap)]
    dot_general x4 -> x0, matrix products: 19.7 us -> none  [the longest x1 16.9 us: shards(): jnp.einsum('qer,qlek->qrlk', unit_blocks, keys, precision=lax.Precision.H...]
    psum x1 -> x0, blocking collectives: 13.4 us -> none  [shards(): squares, prior_total = lax.psum((local_squares, local_total), 'dim')]
    all_to_all x3 -> x8, starting transfers between devices: 33.4 us -> 46.6 us  [the longest x3 22.6 us: over_rows(): return lax.all_to_all(x, 'rows', split_axis=0, concat_axis=0, tiled=True)]
    gather x9 -> x0, local copies, waits for them, and re-layouts: 12.5 us -> none  [the longest x3 4.11 us: shards(): near = came[flat]]
    unnamed x19 -> x32, local copies, waits for them, and re-layouts: 3.41 us -> 7.96 us
  transfers between devices with their start and end apart: 4 -> 13, of which waited for: 2 -> 9; matrix products, arithmetic and copies ran while one was open for 3% -> 2% of each run, Pallas kernels for 0% -> 5%
where the time goes in v1:
time: 266 us; the launch traced here: 265 us
  waiting for transfers between devices  77.7 us (29%)
  blocking collectives  67.8 us (25%)
  starting transfers between devices  67 us (25%)
  Pallas kernels  34.9 us (13%)
  local copies, waits for them, and re-layouts  12.9 us (5%)
  other arithmetic  4.19 us (2%)
    all_to_all x2, blocking collectives, over_rows(): return lax.all_to_all(x, 'rows', split_axis=0, concat_axis=0, tiled=True)  56.7 us
    all_to_all x3, waiting for transfers between devices, over_rows(): return lax.all_to_all(x, 'rows', split_axis=0, concat_axis=0, tiled=True)  55 us
    pallas_call x14, Pallas kernels, call(): pl.pallas_call(body, out_shape=outs, in_specs=specs, out_specs=jax.tree.m...  34.9 us
    all_to_all x3, starting transfers between devices, over_rows(): return lax.all_to_all(x, 'rows', split_axis=0, concat_axis=0, tiled=True)  22.6 us
    ppermute x5, starting transfers between devices, other_core(): return lax.ppermute(x, 'dim', swap)  20.3 us
    all_to_all x4, starting transfers between devices, over_y(): lax.all_to_all(x, 'dim', split_axis=0, concat_axis=0, tiled=True, axis_in...  16.3 us
    all_to_all x1, blocking collectives, over_y(): lax.all_to_all(x, 'dim', split_axis=0, concat_axis=0, tiled=True, axis_in...  11.1 us
    all_to_all x4, waiting for transfers between devices, over_y(): lax.all_to_all(x, 'dim', split_axis=0, concat_axis=0, tiled=True, axis_in...  11.1 us
  transfers between devices with their start and end apart: 13, of which 9 were waited for; matrix products, arithmetic and copies ran while one was open for 2% of the time, Pallas kernels for 5%

profile of v1, /device:TPU:1, one launch (start us, length us, event | category | flops | bytes accessed | tf_op | source)
XLA Modules:
  0.0 264.6 jit_solution(5072185257595036478)
XLA Ops:
  1.6 11.9 %all-to-all-start.1 = ((s32[32,1,2]{2,1,0:T(1,128)}), s32[32,1,2]{2,1,0:T(1,128)S(1)}, u32[]{:S(2)}, u32[]{:S(2)}) async-start(s32[32,1,2]{2,1,0:T(1,128)} %copy.9), calls=%async_computation.1 | async-start | bytes 32768 | tf_op jit(solution)/shard_map/all_to_all | solution.py:308
  14.5 7.6 %all-to-all-done.1 = s32[32,1,2]{2,1,0:T(1,128)S(1)} async-done(((s32[32,1,2]{2,1,0:T(1,128)}), s32[32,1,2]{2,1,0:T(1,128)S(1)}, u32[]{:S(2)}, u32[]{:S(2)}) %all-to-all-start.1) | async-done | bytes 288 | tf_op jit(solution)/shard_map/all_to_all | solution.py:308
  23.0 4.2 %all-to-all-start = ((bf16[4,8,64,128]{3,2,1,0:T(8,128)(2,1)}), bf16[4,8,64,128]{3,2,1,0:T(8,128)(2,1)S(1)}, u32[]{:S(2)}, u32[]{:S(2)}) async-start(bf16[4,8,64,128]{3,2,1,0:T(8,128)(2,1)} %broadcast_in_dim.34), calls=%async_computation | async-start | bytes 1048576 | tf_op jit(solution)/shard_map/all_to_all | solution.py:303
  29.1 5.1 %all-to-all-done.every_ref = bf16[4,8,64,128]{3,2,1,0:T(8,128)(2,1)S(1)} async-done(((bf16[4,8,64,128]{3,2,1,0:T(8,128)(2,1)}), bf16[4,8,64,128]{3,2,1,0:T(8,128)(2,1)S(1)}, u32[]{:S(2)}, u32[]{:S(2)}) %all-to-all-start) | async-done | bytes 524320 | tf_op jit(solution)/shard_map/all_to_all | solution.py:303
  34.9 2.6 shard_map.55
  37.5 25.7 %all_to_all.59 = bf16[32,2,32,256]{3,2,1,0:T(8,128)(2,1)S(1)} all-to-all(bf16[32,2,32,256]{3,2,1,0:T(8,128)(2,1)} %bitcast.29), channel_id=1, replica_groups=mesh['rows'=32,'dim'=8] {'rows'}, dimensions={0} | all-to-all | bytes 2097152 | tf_op jit(solution)/shard_map/all_to_all | solution.py:308
  63.2 8.0 %collective-permute-start.1 = (bf16[64,32,256]{2,1,0:T(8,128)(2,1)S(1)}, bf16[64,32,256]{2,1,0:T(8,128)(2,1)S(1)}, u32[]{:S(2)}, u32[]{:S(2)}) collective-permute-start(bf16[64,32,256]{2,1,0:T(8,128)(2,1)S(1)} %bitcast.23), channel_id=1, source_target_pairs={{0,1},{1,0},{2,3},{3,2},{4,5},{5,4},{6,7},{7,6},{8,9},{9,8},{10,11... | collective-permute-start | bytes 3145736 | tf_op jit(solution)/shard_map/ppermute | solution.py:311
  73.1 3.4 %all-to-all-start.4 = ((f32[4,4,32,128]{3,2,1,0:T(8,128)}), f32[4,4,32,128]{3,2,1,0:T(8,128)S(1)}, u32[]{:S(2)}, u32[]{:S(2)}) async-start(f32[4,4,32,128]{3,2,1,0:T(8,128)} %shard_map.58), calls=%async_computation.4 | async-start | bytes 524288 | tf_op jit(solution)/shard_map/all_to_all | solution.py:303
  78.9 5.0 %shard_map.56 = (f32[8,512,128]{2,1,0:T(8,128)}, f32[8,128]{1,0:T(8,128)}) custom-call(bf16[8,128,256]{2,1,0:T(8,128)(2,1)} %get-tuple-element.15.q_ref, bf16[8,128,256]{2,1,0:T(8,128)(2,1)} %copy-done.10, bf16[64,32,256]{2,1,0:T(8,128)(2,1)} %bitcast.24, bf16[64,32,256]{2,1,0:T(8,128)(2,1)} %copy-done.7, s32[128]{0:T(128)} %fusion.8.flat_ref), custom_call_target="tpu_custom_call" | custom-call | tf_op jit(solution)/shard_map/pallas_call | solution.py:23
  85.2 4.2 %all-to-all-start.3 = ((f32[4,8,128]{2,1,0:T(8,128)}), f32[4,8,128]{2,1,0:T(8,128)S(1)}, u32[]{:S(2)}, u32[]{:S(2)}) async-start(f32[4,8,128]{2,1,0:T(8,128)} %broadcast_in_dim.62), calls=%async_computation.3 | async-start | bytes 32768 | tf_op jit(solution)/shard_map/all_to_all | solution.py:303
  93.8 2.2 shard_map.60
  96.0 4.8 %all-to-all-start.5 = ((bf16[32,2,32,256]{3,2,1,0:T(8,128)(2,1)}), bf16[32,2,32,256]{3,2,1,0:T(8,128)(2,1)S(1)}, u32[]{:S(2)}, u32[]{:S(2)}) async-start(bf16[32,2,32,256]{3,2,1,0:T(8,128)(2,1)} %bitcast.21), calls=%async_computation.5 | async-start | bytes 2097152 | tf_op jit(solution)/shard_map/all_to_all | solution.py:308
  100.9 2.9 %shard_map.57.weights_ref = bf16[8,128,512]{2,1,0:T(8,128)(2,1)} custom-call(f32[8,512,128]{2,1,0:T(8,128)} %get-tuple-element.17.raised_ref, f32[4,8,128]{2,1,0:T(8,128)} %copy-done.11), custom_call_target="tpu_custom_call" | custom-call | tf_op jit(solution)/shard_map/pallas_call | solution.py:23
  103.8 22.2 %all-to-all-done.5 = bf16[32,2,32,256]{3,2,1,0:T(8,128)(2,1)S(1)} async-done(((bf16[32,2,32,256]{3,2,1,0:T(8,128)(2,1)}), bf16[32,2,32,256]{3,2,1,0:T(8,128)(2,1)S(1)}, u32[]{:S(2)}, u32[]{:S(2)}) %all-to-all-start.5) | async-done | bytes 1048608 | tf_op jit(solution)/shard_map/all_to_all | solution.py:308
  127.0 2.8 %shard_map.61 = bf16[4,8,32,256]{3,2,1,0:T(8,128)(2,1)} custom-call(bf16[8,128,512]{2,1,0:T(8,128)(2,1)} %shard_map.57.weights_ref, bf16[64,32,256]{2,1,0:T(8,128)(2,1)} %bitcast.22, s32[128]{0:T(128)} %fusion.8.flat_ref), custom_call_target="tpu_custom_call" | custom-call | tf_op jit(solution)/shard_map/pallas_call | solution.py:23
  129.8 4.5 %all-to-all-start.6 = ((bf16[4,8,32,256]{3,2,1,0:T(8,128)(2,1)}), bf16[4,8,32,256]{3,2,1,0:T(8,128)(2,1)S(1)}, u32[]{:S(2)}, u32[]{:S(2)}) async-start(bf16[4,8,32,256]{3,2,1,0:T(8,128)(2,1)} %shard_map.61), calls=%async_computation.6 | async-start | bytes 1048576 | tf_op jit(solution)/shard_map/all_to_all | solution.py:303
  135.2 6.0 %all-to-all-done.6.parts_ref = bf16[4,8,32,256]{3,2,1,0:T(8,128)(2,1)S(1)} async-done(((bf16[4,8,32,256]{3,2,1,0:T(8,128)(2,1)}), bf16[4,8,32,256]{3,2,1,0:T(8,128)(2,1)S(1)}, u32[]{:S(2)}, u32[]{:S(2)}) %all-to-all-start.6) | async-done | bytes 524320 | tf_op jit(solution)/shard_map/all_to_all | solution.py:303
  142.0 1.9 shard_map.62
  143.9 5.8 %collective-permute-start.3 = (f32[8,256]{1,0:T(8,128)}, f32[8,256]{1,0:T(8,128)S(1)}, u32[]{:S(2)}, u32[]{:S(2)}) collective-permute-start(f32[8,256]{1,0:T(8,128)} %get-tuple-element.22.total_ref), channel_id=1, source_target_pairs={{0,1},{1,0},{2,3},{3,2},{4,5},{5,4},{6,7},{7,6},{8,9},{9,8},{10,11... | collective-permute-start | bytes 24584 | tf_op jit(solution)/shard_map/ppermute | solution.py:311
  151.3 2.2 shard_map.63
  153.5 31.0 %all_to_all.60 = bf16[32,2,32,256]{3,2,1,0:T(8,128)(2,1)} all-to-all(bf16[32,2,32,256]{3,2,1,0:T(8,128)(2,1)} %bitcast.27), channel_id=1, replica_groups=mesh['rows'=32,'dim'=8] {'rows'}, dimensions={0} | all-to-all | bytes 2097152 | tf_op jit(solution)/shard_map/all_to_all | solution.py:308
  184.5 2.8 %shard_map.64 = bf16[4,8,32,256]{3,2,1,0:T(8,128)(2,1)} custom-call(bf16[8,128,512]{2,1,0:T(8,128)(2,1)} %shard_map.57.weights_ref, bf16[64,32,256]{2,1,0:T(8,128)(2,1)} %bitcast.28, s32[128]{0:T(128)} %fusion.8.flat_ref), custom_call_target="tpu_custom_call" | custom-call | tf_op jit(solution)/shard_map/pallas_call | solution.py:23
  187.3 11.1 %all_to_all.61.parts_ref = bf16[4,8,32,256]{3,2,1,0:T(8,128)(2,1)} all-to-all(bf16[4,8,32,256]{3,2,1,0:T(8,128)(2,1)} %shard_map.64), channel_id=1, replica_groups={{0,2,4,6},{1,3,5,7},{8,10,12,14},{9,11,13,15},{16,18,20,22},{17,19,21,2..., dimensions={0} | all-to-all | bytes 1048576 | tf_op jit(solution)/shard_map/all_to_all | solution.py:303
  198.4 1.9 shard_map.65
  200.3 5.5 %collective-permute-start.4 = (f32[8,256]{1,0:T(8,128)}, f32[8,256]{1,0:T(8,128)S(1)}, u32[]{:S(2)}, u32[]{:S(2)}) collective-permute-start(f32[8,256]{1,0:T(8,128)} %get-tuple-element.24.total_ref), channel_id=1, source_target_pairs={{0,1},{1,0},{2,3},{3,2},{4,5},{5,4},{6,7},{7,6},{8,9},{9,8},{10,11... | collective-permute-start | bytes 24584 | tf_op jit(solution)/shard_map/ppermute | solution.py:311
  207.5 2.2 shard_map.66
  209.6 6.0 %all-to-all-start.9 = ((bf16[32,2,32,256]{3,2,1,0:T(8,128)(2,1)}), bf16[32,2,32,256]{3,2,1,0:T(8,128)(2,1)S(1)}, u32[]{:S(2)}, u32[]{:S(2)}) async-start(bf16[32,2,32,256]{3,2,1,0:T(8,128)(2,1)} %bitcast.26), calls=%async_computation.9 | async-start | bytes 2097152 | tf_op jit(solution)/shard_map/all_to_all | solution.py:308
  215.6 25.2 %all-to-all-done.9 = bf16[32,2,32,256]{3,2,1,0:T(8,128)(2,1)S(1)} async-done(((bf16[32,2,32,256]{3,2,1,0:T(8,128)(2,1)}), bf16[32,2,32,256]{3,2,1,0:T(8,128)(2,1)S(1)}, u32[]{:S(2)}, u32[]{:S(2)}) %all-to-all-start.9) | async-done | bytes 1048608 | tf_op jit(solution)/shard_map/all_to_all | solution.py:308
  241.8 2.8 %shard_map.67 = bf16[8,128,256]{2,1,0:T(8,128)(2,1)} custom-call(bf16[8,128,512]{2,1,0:T(8,128)(2,1)} %shard_map.57.weights_ref, bf16[64,32,256]{2,1,0:T(8,128)(2,1)} %bitcast.25, s32[128]{0:T(128)} %fusion.8.flat_ref), custom_call_target="tpu_custom_call" | custom-call | tf_op jit(solution)/shard_map/pallas_call | solution.py:23
  244.6 7.7 %all-to-all-start.10 = ((bf16[8,128,256]{2,1,0:T(8,128)(2,1)}), bf16[8,128,256]{2,1,0:T(8,128)(2,1)S(1)}, u32[]{:S(2)}, u32[]{:S(2)}) async-start(bf16[8,128,256]{2,1,0:T(8,128)(2,1)} %shard_map.67), calls=%async_computation.10 | async-start | bytes 1048576 | tf_op jit(solution)/shard_map/all_to_all | solution.py:365
  253.2 8.5 %all-to-all-done.10.parts_ref = bf16[8,128,256]{2,1,0:T(8,128)(2,1)S(1)} async-done(((bf16[8,128,256]{2,1,0:T(8,128)(2,1)}), bf16[8,128,256]{2,1,0:T(8,128)(2,1)S(1)}, u32[]{:S(2)}, u32[]{:S(2)}) %all-to-all-start.10) | async-done | bytes 524320 | tf_op jit(solution)/shard_map/all_to_all | solution.py:365
  262.5 2.1 shard_map.68
  (65 shorter events, 24.9 us)
Async XLA Ops:
  0.0 100.8 %copy-start = (s32[1024]{0:T(1024)S(1)}, s32[1024]{0:T(1024)}, u32[]{:S(2)}) copy-start(s32[1024]{0:T(1024)} %param.9) | copy-start | bytes 12292
  1.6 20.4 %all-to-all-start.1 = ((s32[32,1,2]{2,1,0:T(1,128)}), s32[32,1,2]{2,1,0:T(1,128)S(1)}, u32[]{:S(2)}, u32[]{:S(2)}) async-start(s32[32,1,2]{2,1,0:T(1,128)} %copy.9), calls=%async_computation.1 | async-start | bytes 32768 | tf_op jit(solution)/shard_map/all_to_all | solution.py:308
  23.0 11.1 %all-to-all-start = ((bf16[4,8,64,128]{3,2,1,0:T(8,128)(2,1)}), bf16[4,8,64,128]{3,2,1,0:T(8,128)(2,1)S(1)}, u32[]{:S(2)}, u32[]{:S(2)}) async-start(bf16[4,8,64,128]{3,2,1,0:T(8,128)(2,1)} %broadcast_in_dim.34), calls=%async_computation | async-start | bytes 1048576 | tf_op jit(solution)/shard_map/all_to_all | solution.py:303
  34.1 0.8 copy-start.4
  37.5 33.7 %copy-start.9 = (bf16[8,128,256]{2,1,0:T(8,128)(2,1)S(1)}, bf16[8,128,256]{2,1,0:T(8,128)(2,1)}, u32[]{:S(2)}) copy-start(bf16[8,128,256]{2,1,0:T(8,128)(2,1)} %get-tuple-element.15.q_ref) | copy-start | bytes 1572868
  63.2 14.0 %copy-start.2 = (bf16[32,2,32,256]{3,2,1,0:T(8,128)(2,1)}, bf16[32,2,32,256]{3,2,1,0:T(8,128)(2,1)S(1)}, u32[]{:S(2)}) copy-start(bf16[32,2,32,256]{3,2,1,0:T(8,128)(2,1)S(1)} %all_to_all.59) | copy-start | bytes 3145732
  63.2 13.9 %collective-permute-start.1 = (bf16[64,32,256]{2,1,0:T(8,128)(2,1)S(1)}, bf16[64,32,256]{2,1,0:T(8,128)(2,1)S(1)}, u32[]{:S(2)}, u32[]{:S(2)}) collective-permute-start(bf16[64,32,256]{2,1,0:T(8,128)(2,1)S(1)} %bitcast.23), channel_id=1, source_target_pairs={{0,1},{1,0},{2,3},{3,2},{4,5},{5,4},{6,7},{7,6},{8,9},{9,8},{10,11... | collective-permute-start | bytes 3145736 | tf_op jit(solution)/shard_map/ppermute | solution.py:311
  71.2 5.9 %collective-permute-start = (bf16[8,128,256]{2,1,0:T(8,128)(2,1)S(1)}, bf16[8,128,256]{2,1,0:T(8,128)(2,1)S(1)}, u32[]{:S(2)}, u32[]{:S(2)}) collective-permute-start(bf16[8,128,256]{2,1,0:T(8,128)(2,1)S(1)} %copy-done.9), channel_id=1, source_target_pairs={{0,1},{1,0},{2,3},{3,2},{4,5},{5,4},{6,7},{7,6},{8,9},{9,8},{10,11... | collective-permute-start | bytes 1572872 | tf_op jit(solution)/shard_map/ppermute | solution.py:311
  73.1 10.8 %all-to-all-start.4 = ((f32[4,4,32,128]{3,2,1,0:T(8,128)}), f32[4,4,32,128]{3,2,1,0:T(8,128)S(1)}, u32[]{:S(2)}, u32[]{:S(2)}) async-start(f32[4,4,32,128]{3,2,1,0:T(8,128)} %shard_map.58), calls=%async_computation.4 | async-start | bytes 524288 | tf_op jit(solution)/shard_map/all_to_all | solution.py:303
  77.1 0.8 copy-start.10
  77.9 1.0 copy-start.7
  83.9 5.5 %copy-start.8 = (f32[4,4,32,128]{3,2,1,0:T(8,128)}, f32[4,4,32,128]{3,2,1,0:T(8,128)S(1)}, u32[]{:S(2)}) copy-start(f32[4,4,32,128]{3,2,1,0:T(8,128)S(1)} %all-to-all-done.4.came_ref) | copy-start | bytes 786436
  85.2 10.8 %all-to-all-start.3 = ((f32[4,8,128]{2,1,0:T(8,128)}), f32[4,8,128]{2,1,0:T(8,128)S(1)}, u32[]{:S(2)}, u32[]{:S(2)}) async-start(f32[4,8,128]{2,1,0:T(8,128)} %broadcast_in_dim.62), calls=%async_computation.3 | async-start | bytes 32768 | tf_op jit(solution)/shard_map/all_to_all | solution.py:303
  91.2 2.0 collective-permute-start.2
  93.2 0.6 copy-start.13
  96.0 4.9 %copy-start.11 = (f32[4,8,128]{2,1,0:T(8,128)}, f32[4,8,128]{2,1,0:T(8,128)S(1)}, u32[]{:S(2)}) copy-start(f32[4,8,128]{2,1,0:T(8,128)S(1)} %all-to-all-done.3.sums_ref) | copy-start | bytes 49156
  96.0 30.0 %all-to-all-start.5 = ((bf16[32,2,32,256]{3,2,1,0:T(8,128)(2,1)}), bf16[32,2,32,256]{3,2,1,0:T(8,128)(2,1)S(1)}, u32[]{:S(2)}, u32[]{:S(2)}) async-start(bf16[32,2,32,256]{3,2,1,0:T(8,128)(2,1)} %bitcast.21), calls=%async_computation.5 | async-start | bytes 2097152 | tf_op jit(solution)/shard_map/all_to_all | solution.py:308
  103.8 30.5 %copy-start.15 = (s32[1024]{0:T(1024)S(1)}, s32[1024]{0:T(1024)}, u32[]{:S(2)}) copy-start(s32[1024]{0:T(1024)} %param.8) | copy-start | bytes 12292
  126.0 1.0 copy-start.1
  129.8 11.5 %all-to-all-start.6 = ((bf16[4,8,32,256]{3,2,1,0:T(8,128)(2,1)}), bf16[4,8,32,256]{3,2,1,0:T(8,128)(2,1)S(1)}, u32[]{:S(2)}, u32[]{:S(2)}) async-start(bf16[4,8,32,256]{3,2,1,0:T(8,128)(2,1)} %shard_map.61), calls=%async_computation.6 | async-start | bytes 1048576 | tf_op jit(solution)/shard_map/all_to_all | solution.py:303
  141.2 0.8 copy-start.6
  143.9 6.8 %collective-permute-start.3 = (f32[8,256]{1,0:T(8,128)}, f32[8,256]{1,0:T(8,128)S(1)}, u32[]{:S(2)}, u32[]{:S(2)}) collective-permute-start(f32[8,256]{1,0:T(8,128)} %get-tuple-element.22.total_ref), channel_id=1, source_target_pairs={{0,1},{1,0},{2,3},{3,2},{4,5},{5,4},{6,7},{7,6},{8,9},{9,8},{10,11... | collective-permute-start | bytes 24584 | tf_op jit(solution)/shard_map/ppermute | solution.py:311
  150.7 0.6 copy-start.14
  200.3 6.5 %collective-permute-start.4 = (f32[8,256]{1,0:T(8,128)}, f32[8,256]{1,0:T(8,128)S(1)}, u32[]{:S(2)}, u32[]{:S(2)}) collective-permute-start(f32[8,256]{1,0:T(8,128)} %get-tuple-element.24.total_ref), channel_id=1, source_target_pairs={{0,1},{1,0},{2,3},{3,2},{4,5},{5,4},{6,7},{7,6},{8,9},{9,8},{10,11... | collective-permute-start | bytes 24584 | tf_op jit(solution)/shard_map/ppermute | solution.py:311
  206.9 0.6 copy-start.12
  209.6 31.2 %all-to-all-start.9 = ((bf16[32,2,32,256]{3,2,1,0:T(8,128)(2,1)}), bf16[32,2,32,256]{3,2,1,0:T(8,128)(2,1)S(1)}, u32[]{:S(2)}, u32[]{:S(2)}) async-start(bf16[32,2,32,256]{3,2,1,0:T(8,128)(2,1)} %bitcast.26), calls=%async_computation.9 | async-start | bytes 2097152 | tf_op jit(solution)/shard_map/all_to_all | solution.py:308
  240.8 1.0 copy-start.3
  244.6 17.1 %all-to-all-start.10 = ((bf16[8,128,256]{2,1,0:T(8,128)(2,1)}), bf16[8,128,256]{2,1,0:T(8,128)(2,1)S(1)}, u32[]{:S(2)}, u32[]{:S(2)}) async-start(bf16[8,128,256]{2,1,0:T(8,128)(2,1)} %shard_map.67), calls=%async_computation.10 | async-start | bytes 1048576 | tf_op jit(solution)/shard_map/all_to_all | solution.py:365
  261.7 0.8 copy-start.5
